TPU v7x, 256 devices: a whole 4x4x8 slice. The times are simulated.
256 devices in a mesh: gx: 32 (over z, x_lo, core), gy: 8 (over y, x_hi).
Axes of the slice: x: 4 (x_hi: 2, x_lo: 2; x = x_hi * 2 + x_lo), y: 4, z: 8, core: 2. Of those that a mesh axis runs over, the one named last changes fastest.
Arguments:
- field: float32 [32, 128, 128, 256], P(None, 'gx', 'gy'), may hold values from -6 to 6
- spec_weight: float32 [2, 32, 32, 32, 32, 32], P(None, None, 'gx', 'gy'), may hold values from -6 to 6
- dw_kernel: float32 [32, 3, 3, 3], replicated, may hold values from -1.25 to 1.25
- point_weight: float32 [32, 32], replicated, may hold values from -1 to 1
- bias: float32 [32], replicated, may hold values from -3 to 3
Outputs:
- evolved: float32 [32, 128, 128, 256], P(None, 'gx', 'gy')
All inputs are finite; a program needn't handle non-finite values.
Results may differ from a plain program's by a relative error of at most 0.00005.
Values sent between devices are 32-bit elements; how exact they have to be, the bound alone decides.
No kernel may reach another device: no remote copies, remote signals or barrier semaphores. Data moves between devices by JAX's collectives and lax.ppermute only.
A program may use at most 128 MiB of HBM per device.

v0:
```python
import jax
import jax.numpy as jnp
from jax import lax
from jax.sharding import PartitionSpec as P

full_turn = 6.283185307179586


def extended(array, sides, width):
    for axis, dim in sides:
        count, length = (lax.axis_size(axis), array.shape[dim])
        up = [(i, (i + 1) % count) for i in range(count)]
        down = [(j, i) for i, j in up]
        last = lax.slice_in_dim(array, length - width, length, axis=dim)
        leading = lax.slice_in_dim(array, 0, width, axis=dim)
        before = lax.ppermute(last, axis, up)
        after = lax.ppermute(leading, axis, down)
        array = jnp.concatenate([before, array, after], axis=dim)
    return array


def kept_index(modes, length):
    index = jnp.arange(modes, dtype=jnp.int32)
    return jnp.where(index < modes // 2, index, index + length - modes)


def phase_table(freqs, positions, length):
    product = freqs[:, None] * positions[None, :] % length
    angle = product.astype(jnp.float32) * (full_turn / length)
    return (jnp.cos(angle), jnp.sin(angle))


def complex_table(cosine, sine_tab, direction):
    upper = jnp.stack([cosine, direction * sine_tab])
    lower = jnp.stack([-direction * sine_tab, cosine])
    return jnp.stack([upper, lower])


def on_device(field, spec_weight, dw_kernel, point_weight, bias):
    exact_mode = lax.Precision.HIGHEST
    chans, rows_x, rows_y, depth = field.shape
    modes = spec_weight.shape[1]
    full_x = rows_x * lax.axis_size("gx")
    full_y = rows_y * lax.axis_size("gy")
    zfreqs = jnp.arange(modes, dtype=jnp.int32)
    zcosine, zsine = phase_table(zfreqs, jnp.arange(depth, dtype=jnp.int32), depth)
    forward_z = jnp.concatenate([zcosine, -zsine], axis=0)
    zspec = jnp.einsum("tz,cxyz->tcxy", forward_z, field, precision=exact_mode).reshape(
        2, modes, chans, rows_x, rows_y
    )
    yfreqs = kept_index(modes, full_y)
    wide = lax.all_to_all(zspec, "gy", split_axis=1, concat_axis=4, tiled=True)
    ycosine, ysine = phase_table(yfreqs, jnp.arange(full_y, dtype=jnp.int32), full_y)
    ytable = complex_table(ycosine, ysine, 1.0)
    yspec = jnp.einsum("srny,rkcxy->snxkc", ytable, wide, precision=exact_mode)
    yspec = yspec.reshape(2, modes, rows_x, -1)
    columns = lax.all_to_all(yspec, "gx", split_axis=1, concat_axis=2, tiled=True)
    xcosine, xsine = phase_table(
        kept_index(modes, full_x), jnp.arange(full_x, dtype=jnp.int32), full_x
    )
    xtable = complex_table(xcosine, xsine, 1.0)
    xspec = jnp.einsum("srma,rnak->snmk", xtable, columns, precision=exact_mode)
    cols_loc = xspec.shape[1]
    xin = xspec.reshape(2, cols_loc, modes, -1, chans)
    weight_re = spec_weight[0]
    weight_im = spec_weight[1]
    stacked = jnp.stack([jnp.stack([weight_re, -weight_im]), jnp.stack([weight_im, weight_re])])
    mixed = jnp.einsum("rnmki,srmnkio->snmko", xin, stacked, precision=exact_mode)
    mixed = mixed.reshape(2, cols_loc, modes, -1)
    xinverse = complex_table(xcosine / full_x, xsine / full_x, -1.0)
    back_x = jnp.einsum("srma,rnmk->snak", xinverse, mixed, precision=exact_mode)
    rows_back = lax.all_to_all(back_x, "gx", split_axis=2, concat_axis=1, tiled=True)
    yinverse = complex_table(ycosine / full_y, ysine / full_y, -1.0)
    tall = jnp.einsum("srnb,rnxk->sbxk", yinverse, rows_back, precision=exact_mode)
    zback = lax.all_to_all(tall, "gy", split_axis=1, concat_axis=3, tiled=True)
    weights_z = jnp.where(zfreqs == 0, 1.0, 2.0).astype(jnp.float32)[:, None] / depth
    backward_z = jnp.stack([weights_z * zcosine, -weights_z * zsine])
    zcells = zback.reshape(2, rows_y, rows_x, modes, chans)
    spectral = jnp.einsum("skz,syxkc->cxyz", backward_z, zcells, precision=exact_mode)
    framed = extended(field, (("gx", 1), ("gy", 2)), 1)
    framed = jnp.concatenate([framed[..., -1:], framed, framed[..., :1]], axis=3)
    conv = jnp.zeros(field.shape, jnp.float32)
    for shift_x in range(3):
        for shift_y in range(3):
            for shift_z in range(3):
                tap = dw_kernel[:, shift_x, shift_y, shift_z][:, None, None, None]
                conv = (
                    conv
                    + tap
                    * framed[
                        :,
                        shift_x : shift_x + rows_x,
                        shift_y : shift_y + rows_y,
                        shift_z : shift_z + depth,
                    ]
                )
    pointwise = jnp.dot(point_weight.T, field.reshape(chans, -1), precision=exact_mode).reshape(
        field.shape
    )
    total = spectral + conv + pointwise + bias[:, None, None, None]
    return jax.nn.gelu(total)


def solution(mesh):
    placed = (P(None, "gx", "gy", None), P(None, None, "gx", "gy", None, None), P(), P(), P())
    return jax.shard_map(
        on_device, mesh=mesh, in_specs=placed, out_specs=P(None, "gx", "gy", None), check_vma=False
    )
```

profile of v0, /device:TPU:1, one launch (start us, length us, event | category | flops | bytes accessed | tf_op | source)
XLA Modules:
  0.0 143.8 jit_solution(5653876701960673272)
XLA Ops:
  0.2 4.2 %fusion.61 = f32[64,32,4,16]{0,1,3,2:T(8,128)S(1)} fusion(f32[32,256]{1,0:T(8,128)S(1)} %get-tuple-element.53, f32[32,256]{1,0:T(8,128)S(1)} %get-tuple-element.54, f32[32,4,16,256]{3,2,1,0:T(8,128)} %param.5), kind=kOutput, calls=%fused_computation.102 | convolution fusion | flops 402669568 | bytes 2686976 | tf_op jit(solution)/shard_map/tz,cxyz->tcxy/dot_general | solution.py:48
  4.4 1.2 reshape.378
  5.6 2.9 %copy.48 = f32[2,32,32,4,16]{2,4,3,0,1:T(8,128)} copy(f32[2,32,32,4,16]{1,0,2,4,3:T(2,128)S(1)} %reshape.378) | data formatting | bytes 1048576 | tf_op jit(solution)/shard_map/reshape | solution.py:48
  8.5 3.3 %reshape.404 = f32[8,1,16384]{2,1,0:T(1,128)} reshape(f32[32,2,4,16,32]{4,3,2,1,0:T(8,128)} %bitcast.180) | data formatting | bytes 1048576
  11.8 7.5 %all-to-all-start = ((f32[8,1,16384]{2,1,0:T(1,128)}), f32[8,1,16384]{2,1,0:T(1,128)S(1)}, u32[]{:S(2)}, u32[]{:S(2)}) async-start(f32[8,1,16384]{2,1,0:T(1,128)} %reshape.404), calls=%async_computation | async-start | bytes 1048576 | tf_op jit(solution)/shard_map/all_to_all | solution.py:52
  19.3 1.2 copy.47
  20.5 1.1 fusion.103
  21.6 1.2 collective-permute-start
  22.9 0.3 slice.210
  23.2 1.2 fusion.100
  24.4 0.7 slice_bitcast_fusion.26
  25.0 2.5 %maximum_bitcast_fusion.1 = f32[1,2,32,1,4,32,32]{6,5,4,2,1,3,0:T(8,128)} fusion(f32[1,32,1,4,32,32]{5,4,3,1,0,2:T(8,128)S(1)} %get-tuple-element.52, f32[1,32,1,4,32,32]{5,4,3,1,0,2:T(8,128)S(1)} %get-tuple-element.5), kind=kLoop, calls=%fused_computation.9 | loop fusion | flops 262144 | bytes 2097152 | tf_op jit(solution)/shard_map/stack | solution.py:67
  27.5 2.5 %maximum_bitcast_fusion.2 = f32[1,2,32,1,4,32,32]{6,5,4,2,1,3,0:T(8,128)} fusion(f32[1,32,1,4,32,32]{5,4,3,2,1,0:T(8,128)S(1)} %get-tuple-element.6, f32[1,32,1,4,32,32]{5,4,3,2,1,0:T(8,128)S(1)} %slice.210), kind=kLoop, calls=%fused_computation.10 | loop fusion | flops 262144 | bytes 2097152 | tf_op jit(solution)/shard_map/stack | solution.py:67
  30.0 0.6 maximum_bitcast_fusion.7
  30.7 0.8 sine_multiply_fusion
  31.5 0.6 broadcast.504
  32.0 1.9 %reduce = f32[8,16384]{1,0:T(8,128)S(1)} reduce(f32[8,1,16384]{2,1,0:T(1,128)S(1)} %all-to-all-done, f32[]{:T(128)} %broadcast.504), dimensions={1}, to_apply=%all_to_all.40.reduce_sub_computation | reduce | bytes 1048580 | tf_op jit(solution)/shard_map/all_to_all | solution.py:52
  34.0 2.0 %reshape.405 = f32[32,2,4,16,32]{4,3,2,1,0:T(8,128)} reshape(f32[8,16384]{1,0:T(8,128)S(1)} %reduce) | data formatting | bytes 1048576
  36.0 1.8 %copy.50 = f32[2,4,32,4,8,16]{2,5,4,3,1,0:T(8,128)S(1)} copy(f32[2,4,32,4,8,16]{2,5,3,0,1,4:T(8,128)} %bitcast.181) | data formatting | bytes 1048576 | tf_op jit(solution)/shard_map/all_to_all | solution.py:52
  37.8 3.5 %fusion.55 = f32[2,32,4,4,32]{1,4,0,2,3:T(8,128)S(1)} fusion(f32[2,4,32,4,128,1]{2,4,3,1,0,5:T(8,128)S(1)} %bitcast.182, f32[1,2,32,128]{3,2,1,0:T(8,128)S(1)} %get-tuple-element.55, f32[1,2,32,128]{3,2,1,0:T(8,128)S(1)} %get-tuple-element.56), kind=kOutput, calls=%fused_computation.91 | convolution fusion | flops 100679680 | bytes 720896 | tf_op jit(solution)/shard_map/srny,rkcxy->snxkc/dot_general | solution.py:55
  41.3 0.6 copy.88
  41.9 1.0 reshape.401
  42.8 14.5 %all-to-all-start.1 = ((f32[2,32,4,128]{3,2,0,1:T(4,128)}), f32[2,32,4,128]{3,2,0,1:T(4,128)S(1)}, u32[]{:S(2)}, u32[]{:S(2)}) async-start(f32[2,32,4,128]{3,2,0,1:T(4,128)} %reshape.401), calls=%async_computation.1 | async-start | bytes 262144 | tf_op jit(solution)/shard_map/all_to_all | solution.py:57
  57.3 1.1 constant_dynamic-update-slice_fusion.2
  58.4 1.2 constant_dynamic-update-slice_fusion.1
  59.6 1.1 constant_dynamic-update-slice_fusion
  60.7 1.7 %copy-done.2 = f32[32,6,16,256]{3,0,2,1:T(8,128)} copy-done((f32[32,6,16,256]{3,0,2,1:T(8,128)}, f32[32,6,16,256]{3,0,2,1:T(8,128)S(1)}, u32[]{:S(2)}) %copy-start.2) | copy-done | bytes 3145752
  62.5 1.1 collective-permute-start.2
  63.6 4.0 %collective-permute-start.3 = (f32[32,6,1,256]{3,0,2,1:T(8,128)S(1)}, f32[32,6,1,256]{3,0,2,1:T(8,128)S(1)}, u32[]{:S(2)}, u32[]{:S(2)}) collective-permute-start(f32[32,6,1,256]{3,0,2,1:T(8,128)S(1)} %get-tuple-element.12), channel_id=1, source_target_pairs={{1,0},{2,1},{3,2},{4,3},{5,4},{6,5},{7,6},{0,7},{9,8},{10,9},{11,1... | collective-permute-start | bytes 589832 | tf_op jit(solution)/shard_map/ppermute | solution.py:17
  67.7 0.2 convolution_bitcast_fusion.2
  68.1 7.2 %fusion = f32[32,4,1,2,32,1]{4,2,5,3,1,0:T(1,128)S(1)} fusion(f32[2,32,4,32,1,1]{3,2,1,0,4,5:T(4,128)S(1)} %reshape.391, f32[1,2,32,1,4,32,32]{6,5,4,2,1,3,0:T(8,128)} %maximum_bitcast_fusion.2, f32[1,2,32,1,4,32,32]{6,5,4,2,1,3,0:T(8,128)} %maximum_bitcast_fusion.1), kind=kOutput, calls=%fused_computation.1 | convolution fusion | flops 6815744 | bytes 2162688 | tf_op jit(solution)/shard_map/rnmki,srmnkio->snmko/dot_general | solution.py:68
  75.5 0.3 convolution_bitcast_fusion.1
  75.8 0.8 copy.55
  76.6 8.8 %all-to-all-start.2 = ((f32[2,1,128,128]{3,0,1,2:T(2,128)}), f32[2,1,128,128]{3,0,1,2:T(2,128)S(1)}, u32[]{:S(2)}, u32[]{:S(2)}) async-start(f32[2,1,128,128]{3,0,1,2:T(2,128)} %copy.55), calls=%async_computation.2 | async-start | bytes 262144 | tf_op jit(solution)/shard_map/all_to_all | solution.py:72
  85.4 1.4 slice_bitcast_fusion.25
  86.9 4.1 %pad_maximum_fusion.1 = f32[32,6,18,256]{3,0,2,1:T(8,128)} fusion(f32[32,6,1,256]{3,0,2,1:T(8,128)S(1)} %collective-permute-done.3, f32[32,6,16,256]{3,0,2,1:T(8,128)} %copy-done.2, f32[32,6,1,256]{3,0,2,1:T(8,128)S(1)} %collective-permute-done.2), kind=kLoop, calls=%fused_computation.11 | loop fusion | flops 1769472 | bytes 7077888 | tf_op jit(solution)/shard_map/concatenate | solution.py:18
  91.0 3.7 %all-to-all-done.2 = f32[2,1,128,128]{3,0,1,2:T(2,128)S(1)} async-done(((f32[2,1,128,128]{3,0,1,2:T(2,128)}), f32[2,1,128,128]{3,0,1,2:T(2,128)S(1)}, u32[]{:S(2)}, u32[]{:S(2)}) %all-to-all-start.2) | async-done | bytes 131104 | tf_op jit(solution)/shard_map/all_to_all | solution.py:72
  94.7 0.6 convolution_bitcast_fusion
  95.3 1.2 copy.58
  96.5 3.5 %all-to-all-start.3 = ((f32[2,128,4,128]{3,2,0,1:T(4,128)}), f32[2,128,4,128]{3,2,0,1:T(4,128)S(1)}, u32[]{:S(2)}, u32[]{:S(2)}) async-start(f32[2,128,4,128]{3,2,0,1:T(4,128)} %copy.58), calls=%async_computation.3 | async-start | bytes 1048576 | tf_op jit(solution)/shard_map/all_to_all | solution.py:75
  100.0 2.8 %fusion.101 = (f32[32,6,18,1]{3,0,2,1:T(8,128)S(1)}, f32[32,6,18,1]{3,0,2,1:T(8,128)S(1)}) fusion(f32[32,6,18,256]{3,0,2,1:T(8,128)} %pad_maximum_fusion.1), kind=kLoop, calls=%fused_computation.197 | loop fusion | bytes 55296 | tf_op jit(solution)/shard_map/slice | solution.py:81
  102.9 5.5 %maximum_maximum_fusion = (f32[32,6,18,257]{3,0,2,1:T(8,128)}, f32[32,6,18,257]{3,0,2,1:T(8,128)}) fusion(f32[32,6,1,256]{3,0,2,1:T(8,128)S(1)} %collective-permute-done.3, f32[32,6,16,256]{3,0,2,1:T(8,128)S(1)} %copy-done.3, f32[32,6,1,256]{3,0,2,1:T(8,128)S(1)} %collective-permute-done.2, f32[32,6,18,1]{3,0,2,1:T(8,128)S(1)} %get-tuple-element.9, ...), kind=kLoop, calls=%fused_computation.3 | loop fusion | flops 5329152 | bytes 10672128 | tf_op jit(solution)/shard_map/concatenate | solution.py:81
  108.4 2.3 %all-to-all-done.3 = f32[2,128,4,128]{3,2,0,1:T(4,128)S(1)} async-done(((f32[2,128,4,128]{3,2,0,1:T(4,128)}), f32[2,128,4,128]{3,2,0,1:T(4,128)S(1)}, u32[]{:S(2)}, u32[]{:S(2)}) %all-to-all-start.3) | async-done | bytes 524320 | tf_op jit(solution)/shard_map/all_to_all | solution.py:75
  110.7 0.3 copy.119
  111.0 1.8 %reshape.383 = f32[2,16,4,32,32]{4,3,2,1,0:T(8,128)} reshape(f32[2,16,4,8,128]{4,3,2,1,0:T(8,128)S(1)} %bitcast.183) | data formatting | bytes 1048576 | tf_op jit(solution)/shard_map/reshape | solution.py:78
  113.1 5.3 %fusion.64 = f32[16,4,32,256,1]{3,2,1,0,4:T(8,128)S(1)} fusion(f32[2,16,4,32,32]{4,3,2,1,0:T(8,128)} %reshape.383, f32[1,32,256]{2,1,0:T(8,128)} %get-tuple-element.57, f32[1,32,256]{2,1,0:T(8,128)} %get-tuple-element.58), kind=kOutput, calls=%fused_computation.107 | convolution fusion | flops 402669568 | bytes 2686976 | tf_op jit(solution)/shard_map/skz,syxkc->cxyz/dot_general | solution.py:79
  118.7 22.6 %fusion.8 = f32[32,4,16,256]{3,0,2,1:T(8,128)S(1)} fusion(f32[32,6,18,257]{3,0,2,1:T(8,128)} %get-tuple-element.8, f32[32,6,1,256]{3,0,2,1:T(8,128)S(1)} %collective-permute-done.3, f32[32,6,16,256]{3,0,2,1:T(8,128)S(1)} %copy-done.4, f32[32,6,18,257]{3,0,2,1:T(8,128)} %get-tuple-element.7, f32[32,1,16,256]{3,0,2,1:T(8,128)} %collective-permute-done.1, ...), kind=kOutput, calls=%fused_computation.23 | convolution fusion | flops 239075328 | bytes 50732544 | tf_op jit(solution)/shard_map/dot_general | solution.py:97
  141.3 2.5 %copy.69 = f32[32,4,16,256]{3,2,1,0:T(8,128)} copy(f32[32,4,16,256]{3,0,2,1:T(8,128)S(1)} %fusion.8) | data formatting | bytes 4194304 | tf_op jit(solution)/shard_map/mul | solution.py:101
  (100 shorter events, 1.0 us)
Async XLA Ops:
  0.0 118.4 %copy-start = (f32[32,32]{1,0:T(8,128)S(1)}, f32[32,32]{1,0:T(8,128)}, u32[]{:S(2)}) copy-start(f32[32,32]{1,0:T(8,128)} %param.8) | copy-start | bytes 12292
  8.5 10.7 %copy-start.1 = (f32[32,4,16,256]{3,2,1,0:T(8,128)S(1)}, f32[32,4,16,256]{3,2,1,0:T(8,128)}, u32[]{:S(2)}) copy-start(f32[32,4,16,256]{3,2,1,0:T(8,128)} %param.5) | copy-start | bytes 6291460
  11.8 19.7 %all-to-all-start = ((f32[8,1,16384]{2,1,0:T(1,128)}), f32[8,1,16384]{2,1,0:T(1,128)S(1)}, u32[]{:S(2)}, u32[]{:S(2)}) async-start(f32[8,1,16384]{2,1,0:T(1,128)} %reshape.404), calls=%async_computation | async-start | bytes 1048576 | tf_op jit(solution)/shard_map/all_to_all | solution.py:52
  19.3 3.6 %copy-start.5 = (f32[2,32,1,4,32,32]{5,4,3,2,1,0:T(8,128)S(1)}, f32[2,32,1,4,32,32]{5,4,3,2,1,0:T(8,128)}, u32[]{:S(2)}) copy-start(f32[2,32,1,4,32,32]{5,4,3,2,1,0:T(8,128)} %param.6) | copy-start | bytes 3145732
  20.5 2.7 %copy-start.6 = (f32[32,4,16,256]{3,0,2,1:T(8,128)}, f32[32,4,16,256]{3,0,2,1:T(8,128)S(1)}, u32[]{:S(2)}) copy-start(f32[32,4,16,256]{3,0,2,1:T(8,128)S(1)} %copy.47) | copy-start | bytes 6291460
  21.6 35.7 %collective-permute-start = (f32[32,1,16,256]{3,0,2,1:T(8,128)}, f32[32,1,16,256]{3,0,2,1:T(8,128)}, u32[]{:S(2)}, u32[]{:S(2)}) collective-permute-start(f32[32,1,16,256]{3,0,2,1:T(8,128)} %get-tuple-element.14), channel_id=1, source_target_pairs={{0,8},{8,16},{16,24},{24,32},{32,40},{40,48},{48,56},{56,64},{64,7... | collective-permute-start | bytes 1572872 | tf_op jit(solution)/shard_map/ppermute | solution.py:16
  22.7 36.9 %collective-permute-start.1 = (f32[32,1,16,256]{3,0,2,1:T(8,128)}, f32[32,1,16,256]{3,0,2,1:T(8,128)}, u32[]{:S(2)}, u32[]{:S(2)}) collective-permute-start(f32[32,1,16,256]{3,0,2,1:T(8,128)} %get-tuple-element.13), channel_id=1, source_target_pairs={{8,0},{16,8},{24,16},{32,24},{40,32},{48,40},{56,48},{64,56},{72,6... | collective-permute-start | bytes 1572872 | tf_op jit(solution)/shard_map/ppermute | solution.py:17
  30.7 7.1 %copy-start.7 = (f32[1,2,32,128]{3,2,1,0:T(8,128)}, f32[1,2,32,128]{3,2,1,0:T(8,128)S(1)}, u32[]{:S(2)}) copy-start(f32[1,2,32,128]{3,2,1,0:T(8,128)S(1)} %get-tuple-element.55) | copy-start | bytes 98308
  30.7 7.2 %copy-start.9 = (f32[1,2,32,128]{3,2,1,0:T(8,128)}, f32[1,2,32,128]{3,2,1,0:T(8,128)S(1)}, u32[]{:S(2)}) copy-start(f32[1,2,32,128]{3,2,1,0:T(8,128)S(1)} %get-tuple-element.56) | copy-start | bytes 98308
  42.8 24.8 %all-to-all-start.1 = ((f32[2,32,4,128]{3,2,0,1:T(4,128)}), f32[2,32,4,128]{3,2,0,1:T(4,128)S(1)}, u32[]{:S(2)}, u32[]{:S(2)}) async-start(f32[2,32,4,128]{3,2,0,1:T(4,128)} %reshape.401), calls=%async_computation.1 | async-start | bytes 262144 | tf_op jit(solution)/shard_map/all_to_all | solution.py:57
  59.6 8.1 %copy-start.8 = (f32[1,2,32,128]{3,2,1,0:T(8,128)S(1)}, f32[1,2,32,128]{3,2,1,0:T(8,128)}, u32[]{:S(2)}) copy-start(f32[1,2,32,128]{3,2,1,0:T(8,128)} %copy-done.7) | copy-start | bytes 98308
  59.6 8.1 %copy-start.10 = (f32[1,2,32,128]{3,2,1,0:T(8,128)S(1)}, f32[1,2,32,128]{3,2,1,0:T(8,128)}, u32[]{:S(2)}) copy-start(f32[1,2,32,128]{3,2,1,0:T(8,128)} %copy-done.9) | copy-start | bytes 98308
  62.5 24.3 %collective-permute-start.2 = (f32[32,6,1,256]{3,0,2,1:T(8,128)S(1)}, f32[32,6,1,256]{3,0,2,1:T(8,128)S(1)}, u32[]{:S(2)}, u32[]{:S(2)}) collective-permute-start(f32[32,6,1,256]{3,0,2,1:T(8,128)S(1)} %get-tuple-element.11), channel_id=1, source_target_pairs={{0,1},{1,2},{2,3},{3,4},{4,5},{5,6},{6,7},{7,0},{8,9},{9,10},{10,1... | collective-permute-start | bytes 589832 | tf_op jit(solution)/shard_map/ppermute | solution.py:16
  63.6 23.2 %collective-permute-start.3 = (f32[32,6,1,256]{3,0,2,1:T(8,128)S(1)}, f32[32,6,1,256]{3,0,2,1:T(8,128)S(1)}, u32[]{:S(2)}, u32[]{:S(2)}) collective-permute-start(f32[32,6,1,256]{3,0,2,1:T(8,128)S(1)} %get-tuple-element.12), channel_id=1, source_target_pairs={{1,0},{2,1},{3,2},{4,3},{5,4},{6,5},{7,6},{0,7},{9,8},{10,9},{11,1... | collective-permute-start | bytes 589832 | tf_op jit(solution)/shard_map/ppermute | solution.py:17
  68.0 7.4 %copy-start.11 = (f32[1,2,32,128]{3,2,1,0:T(8,128)S(1)}, f32[1,2,32,128]{3,2,1,0:T(8,128)}, u32[]{:S(2)}) copy-start(f32[1,2,32,128]{3,2,1,0:T(8,128)} %get-tuple-element.42) | copy-start | bytes 98308
  68.1 7.4 %copy-start.12 = (f32[1,2,32,128]{3,2,1,0:T(8,128)S(1)}, f32[1,2,32,128]{3,2,1,0:T(8,128)}, u32[]{:S(2)}) copy-start(f32[1,2,32,128]{3,2,1,0:T(8,128)} %get-tuple-element.43) | copy-start | bytes 98308
  76.6 18.1 %all-to-all-start.2 = ((f32[2,1,128,128]{3,0,1,2:T(2,128)}), f32[2,1,128,128]{3,0,1,2:T(2,128)S(1)}, u32[]{:S(2)}, u32[]{:S(2)}) async-start(f32[2,1,128,128]{3,0,1,2:T(2,128)} %copy.55), calls=%async_computation.2 | async-start | bytes 262144 | tf_op jit(solution)/shard_map/all_to_all | solution.py:72
  96.5 14.2 %all-to-all-start.3 = ((f32[2,128,4,128]{3,2,0,1:T(4,128)}), f32[2,128,4,128]{3,2,0,1:T(4,128)S(1)}, u32[]{:S(2)}, u32[]{:S(2)}) async-start(f32[2,128,4,128]{3,2,0,1:T(4,128)} %copy.58), calls=%async_computation.3 | async-start | bytes 1048576 | tf_op jit(solution)/shard_map/all_to_all | solution.py:75
  100.0 3.0 %copy-start.3 = (f32[32,6,16,256]{3,0,2,1:T(8,128)S(1)}, f32[32,6,16,256]{3,0,2,1:T(8,128)}, u32[]{:S(2)}) copy-start(f32[32,6,16,256]{3,0,2,1:T(8,128)} %copy-done.2) | copy-start | bytes 9437188
  112.8 5.6 %copy-start.4 = (f32[32,6,16,256]{3,0,2,1:T(8,128)S(1)}, f32[32,6,16,256]{3,0,2,1:T(8,128)}, u32[]{:S(2)}) copy-start(f32[32,6,16,256]{3,0,2,1:T(8,128)} %copy-done.2) | copy-start | bytes 9437188
  112.8 5.6 %copy-start.14 = (f32[32]{0:T(128)S(1)}, f32[32]{0:T(128)}, u32[]{:S(2)}) copy-start(f32[32]{0:T(128)} %get-tuple-element.15) | copy-start | bytes 388
  112.8 5.6 %copy-start.15 = (f32[32]{0:T(128)S(1)}, f32[32]{0:T(128)}, u32[]{:S(2)}) copy-start(f32[32]{0:T(128)} %get-tuple-element.16) | copy-start | bytes 388
  112.8 5.6 %copy-start.16 = (f32[32]{0:T(128)S(1)}, f32[32]{0:T(128)}, u32[]{:S(2)}) copy-start(f32[32]{0:T(128)} %get-tuple-element.17) | copy-start | bytes 388
  112.8 5.6 %copy-start.17 = (f32[32]{0:T(128)S(1)}, f32[32]{0:T(128)}, u32[]{:S(2)}) copy-start(f32[32]{0:T(128)} %get-tuple-element.18) | copy-start | bytes 388
  112.8 5.6 %copy-start.18 = (f32[32]{0:T(128)S(1)}, f32[32]{0:T(128)}, u32[]{:S(2)}) copy-start(f32[32]{0:T(128)} %get-tuple-element.19) | copy-start | bytes 388
  112.8 5.6 %copy-start.19 = (f32[32]{0:T(128)S(1)}, f32[32]{0:T(128)}, u32[]{:S(2)}) copy-start(f32[32]{0:T(128)} %get-tuple-element.20) | copy-start | bytes 388
  112.8 5.6 %copy-start.20 = (f32[32]{0:T(128)S(1)}, f32[32]{0:T(128)}, u32[]{:S(2)}) copy-start(f32[32]{0:T(128)} %get-tuple-element.21) | copy-start | bytes 388
  112.9 5.6 %copy-start.21 = (f32[32]{0:T(128)S(1)}, f32[32]{0:T(128)}, u32[]{:S(2)}) copy-start(f32[32]{0:T(128)} %get-tuple-element.22) | copy-start | bytes 388
  112.9 5.6 %copy-start.22 = (f32[32]{0:T(128)S(1)}, f32[32]{0:T(128)}, u32[]{:S(2)}) copy-start(f32[32]{0:T(128)} %get-tuple-element.23) | copy-start | bytes 388
  112.9 5.6 %copy-start.23 = (f32[32]{0:T(128)S(1)}, f32[32]{0:T(128)}, u32[]{:S(2)}) copy-start(f32[32]{0:T(128)} %get-tuple-element.24) | copy-start | bytes 388
  112.9 5.6 %copy-start.24 = (f32[32]{0:T(128)S(1)}, f32[32]{0:T(128)}, u32[]{:S(2)}) copy-start(f32[32]{0:T(128)} %get-tuple-element.25) | copy-start | bytes 388
  112.9 5.6 %copy-start.25 = (f32[32]{0:T(128)S(1)}, f32[32]{0:T(128)}, u32[]{:S(2)}) copy-start(f32[32]{0:T(128)} %get-tuple-element.26) | copy-start | bytes 388
  112.9 5.6 %copy-start.26 = (f32[32]{0:T(128)S(1)}, f32[32]{0:T(128)}, u32[]{:S(2)}) copy-start(f32[32]{0:T(128)} %get-tuple-element.27) | copy-start | bytes 388
  112.9 5.6 %copy-start.27 = (f32[32]{0:T(128)S(1)}, f32[32]{0:T(128)}, u32[]{:S(2)}) copy-start(f32[32]{0:T(128)} %get-tuple-element.28) | copy-start | bytes 388
  112.9 5.6 %copy-start.28 = (f32[32]{0:T(128)S(1)}, f32[32]{0:T(128)}, u32[]{:S(2)}) copy-start(f32[32]{0:T(128)} %get-tuple-element.29) | copy-start | bytes 388
  112.9 5.6 %copy-start.29 = (f32[32]{0:T(128)S(1)}, f32[32]{0:T(128)}, u32[]{:S(2)}) copy-start(f32[32]{0:T(128)} %get-tuple-element.30) | copy-start | bytes 388
  112.9 5.6 %copy-start.30 = (f32[32]{0:T(128)S(1)}, f32[32]{0:T(128)}, u32[]{:S(2)}) copy-start(f32[32]{0:T(128)} %get-tuple-element.31) | copy-start | bytes 388
  113.0 5.6 %copy-start.31 = (f32[32]{0:T(128)S(1)}, f32[32]{0:T(128)}, u32[]{:S(2)}) copy-start(f32[32]{0:T(128)} %get-tuple-element.32) | copy-start | bytes 388
  113.0 5.6 %copy-start.32 = (f32[32]{0:T(128)S(1)}, f32[32]{0:T(128)}, u32[]{:S(2)}) copy-start(f32[32]{0:T(128)} %get-tuple-element.33) | copy-start | bytes 388
  113.0 5.6 %copy-start.33 = (f32[32]{0:T(128)S(1)}, f32[32]{0:T(128)}, u32[]{:S(2)}) copy-start(f32[32]{0:T(128)} %get-tuple-element.34) | copy-start | bytes 388
  113.0 5.6 %copy-start.34 = (f32[32]{0:T(128)S(1)}, f32[32]{0:T(128)}, u32[]{:S(2)}) copy-start(f32[32]{0:T(128)} %get-tuple-element.35) | copy-start | bytes 388
  113.0 5.6 %copy-start.35 = (f32[32]{0:T(128)S(1)}, f32[32]{0:T(128)}, u32[]{:S(2)}) copy-start(f32[32]{0:T(128)} %get-tuple-element.36) | copy-start | bytes 388
  113.0 5.6 %copy-start.36 = (f32[32]{0:T(128)S(1)}, f32[32]{0:T(128)}, u32[]{:S(2)}) copy-start(f32[32]{0:T(128)} %get-tuple-element.37) | copy-start | bytes 388
  113.0 5.6 %copy-start.37 = (f32[32]{0:T(128)S(1)}, f32[32]{0:T(128)}, u32[]{:S(2)}) copy-start(f32[32]{0:T(128)} %get-tuple-element.38) | copy-start | bytes 388
  113.0 5.6 %copy-start.38 = (f32[32]{0:T(128)S(1)}, f32[32]{0:T(128)}, u32[]{:S(2)}) copy-start(f32[32]{0:T(128)} %get-tuple-element.39) | copy-start | bytes 388
  113.0 5.6 %copy-start.39 = (f32[32]{0:T(128)S(1)}, f32[32]{0:T(128)}, u32[]{:S(2)}) copy-start(f32[32]{0:T(128)} %get-tuple-element.40) | copy-start | bytes 388
  113.0 5.6 %copy-start.40 = (f32[32]{0:T(128)S(1)}, f32[32]{0:T(128)}, u32[]{:S(2)}) copy-start(f32[32]{0:T(128)} %get-tuple-element.41) | copy-start | bytes 388
  113.1 5.6 %copy-start.41 = (f32[32]{0:T(128)S(1)}, f32[32]{0:T(128)}, u32[]{:S(2)}) copy-start(f32[32]{0:T(128)} %param.9) | copy-start | bytes 388
  (2 other events, 2.9 us)
where the time goes:
time: 144 us
  matrix products  44 us (31%)
  starting transfers between devices  40.6 us (28%)
  local copies, waits for them, and re-layouts  33 us (23%)
  other arithmetic  19.4 us (13%)
  waiting for transfers between devices  6 us (4%)
    dot_general x1, matrix products, on_device(): jnp.dot(point_weight.T, field.reshape(chans, -1), precision=exact_mode)  22.6 us
    all_to_all x1, starting transfers between devices, on_device(): lax.all_to_all(yspec, 'gx', split_axis=1, concat_axis=2, tiled=True)  14.5 us
    unnamed x89, local copies, waits for them, and re-layouts  10.9 us
    all_to_all x1, starting transfers between devices, on_device(): lax.all_to_all(back_x, 'gx', split_axis=2, concat_axis=1, tiled=True)  8.83 us
    all_to_all x1, starting transfers between devices, on_device(): wide = lax.all_to_all(zspec, 'gy', split_axis=1, concat_axis=4, tiled=True)  7.48 us
    dot_general x1, matrix products, on_device(): jnp.einsum('rnmki,srmnkio->snmko', xin, stacked, precision=exact_mode)  7.24 us
    concatenate x1, other arithmetic, on_device(): jnp.concatenate([framed[..., -1:], framed, framed[..., :1]], axis=3)  5.5 us
    dot_general x1, matrix products, on_device(): jnp.einsum('skz,syxkc->cxyz', backward_z, zcells, precision=exact_mode)  5.29 us
  transfers between devices with their start and end apart: 8, of which 2 were waited for; matrix products, arithmetic and copies ran while one was open for 34% of the time, Pallas kernels for 0%

commit v1 on v0

--- a/solution.py
+++ b/solution.py
@@ -4,6 +4,12 @@
 from jax.sharding import PartitionSpec as P
 
 full_turn = 6.283185307179586
+
+
+def stacked_exchange(x, mesh_axis, split, join):
+    parts = jnp.split(x, lax.axis_size(mesh_axis), axis=split)
+    received = lax.all_to_all(jnp.stack(parts), mesh_axis, 0, 0)
+    return jnp.concatenate(received, axis=join)
 
 
 def extended(array, sides, width):
@@ -49,7 +55,7 @@
         2, modes, chans, rows_x, rows_y
     )
     yfreqs = kept_index(modes, full_y)
-    wide = lax.all_to_all(zspec, "gy", split_axis=1, concat_axis=4, tiled=True)
+    wide = stacked_exchange(zspec, "gy", 1, 4)
     ycosine, ysine = phase_table(yfreqs, jnp.arange(full_y, dtype=jnp.int32), full_y)
     ytable = complex_table(ycosine, ysine, 1.0)
     yspec = jnp.einsum("srny,rkcxy->snxkc", ytable, wide, precision=exact_mode)

time: 144 us -> 148 us (1.028)
  local copies, waits for them, and re-layouts: 33 us -> 37.7 us
    unnamed x89 -> x98, local copies, waits for them, and re-layouts: 10.9 us -> 15.8 us
    reshape x2 -> x1, local copies, waits for them, and re-layouts: 4.11 us -> 1.91 us  [on_device(): jnp.einsum('tz,cxyz->tcxy', forward_z, field, precision=exact_mode)]
    reshape x0 -> x2, local copies, waits for them, and re-layouts: none -> 2 us  [stacked_exchange(): return jnp.concatenate(received, axis=join)]
    another operation x2 -> x3, local copies, waits for them, and re-layouts: 0.23 us -> 2.05 us  [the longest x1 1.82 us: stacked_exchange(): received = lax.all_to_all(jnp.stack(parts), mesh_axis, 0, 0)]
    all_to_all x2 -> x1, local copies, waits for them, and re-layouts: 2.41 us -> 0.61 us  [stacked_exchange(): received = lax.all_to_all(jnp.stack(parts), mesh_axis, 0, 0)]
  transfers between devices with their start and end apart: 8 -> 8, of which waited for: 2 -> 2; matrix products, arithmetic and copies ran while one was open for 34% -> 33% of each run, Pallas kernels for 0% -> 0%
where the time goes in v1:
time: 148 us
  matrix products  43.1 us (29%)
  starting transfers between devices  40.6 us (27%)
  local copies, waits for them, and re-layouts  37.7 us (25%)
  other arithmetic  19.4 us (13%)
  waiting for transfers between devices  6.02 us (4%)
    dot_general x1, matrix products, on_device(): jnp.dot(point_weight.T, field.reshape(chans, -1), precision=exact_mode)  21.7 us
    unnamed x98, local copies, waits for them, and re-layouts  15.8 us
    all_to_all x1, starting transfers between devices, on_device(): lax.all_to_all(yspec, 'gx', split_axis=1, concat_axis=2, tiled=True)  14.4 us
    all_to_all x1, starting transfers between devices, on_device(): lax.all_to_all(back_x, 'gx', split_axis=2, concat_axis=1, tiled=True)  8.83 us
    all_to_all x1, starting transfers between devices, stacked_exchange(): received = lax.all_to_all(jnp.stack(parts), mesh_axis, 0, 0)  7.48 us
    dot_general x1, matrix products, on_device(): jnp.einsum('rnmki,srmnkio->snmko', xin, stacked, precision=exact_mode)  7.24 us
    concatenate x1, other arithmetic, on_device(): jnp.concatenate([framed[..., -1:], framed, framed[..., :1]], axis=3)  5.49 us
    dot_general x1, matrix products, on_device(): jnp.einsum('skz,syxkc->cxyz', backward_z, zcells, precision=exact_mode)  5.29 us
  transfers between devices with their start and end apart: 8, of which 2 were waited for; matrix products, arithmetic and copies ran while one was open for 33% of the time, Pallas kernels for 0%

profile of v1, /device:TPU:1, one launch (start us, length us, event | category | flops | bytes accessed | tf_op | source)
XLA Modules:
  0.0 147.6 jit_solution(14081820207444335215)
XLA Ops:
  0.2 4.2 %fusion.69 = f32[64,32,4,16]{0,1,3,2:T(8,128)S(1)} fusion(f32[32,256]{1,0:T(8,128)S(1)} %get-tuple-element.53, f32[32,256]{1,0:T(8,128)S(1)} %get-tuple-element.54, f32[32,4,16,256]{3,2,1,0:T(8,128)} %param.5), kind=kOutput, calls=%fused_computation.118 | convolution fusion | flops 402669568 | bytes 2686976 | tf_op jit(solution)/shard_map/tz,cxyz->tcxy/dot_general | solution.py:54
  4.4 1.9 %copy.103 = f32[64,32,4,16]{1,3,2,0:T(8,128)S(1)} copy(f32[64,32,4,16]{0,1,3,2:T(8,128)S(1)} %fusion.69) | data formatting | bytes 1048576 | tf_op jit(solution)/shard_map/reshape | solution.py:54
  6.3 0.8 fusion.65
  7.1 0.8 fusion.64
  7.8 0.7 fusion.63
  8.6 0.7 fusion.62
  9.3 0.7 fusion.61
  10.0 0.7 fusion.60
  10.7 0.7 fusion.59
  11.4 1.8 %fusion.58 = f32[8,2,4,32,4,16]{3,5,4,2,1,0:T(8,128)} fusion(f32[8,2,4,32,4,16]{3,5,4,2,1,0:T(8,128)} %fusion.59, f32[2,32,32,4,16]{2,4,3,1,0:T(8,128)} %bitcast.216), kind=kLoop, calls=%fused_computation.97 | loop fusion | bytes 524288 | tf_op jit(solution)/shard_map/stack | solution.py:11
  13.3 3.1 %reshape.412 = f32[8,1,16384]{2,1,0:T(1,128)} reshape(f32[8,2,4,4,16,32]{5,4,3,2,1,0:T(8,128)} %bitcast.196) | data formatting | bytes 1048576
  16.4 7.5 %all-to-all-start = ((f32[8,1,16384]{2,1,0:T(1,128)}), f32[8,1,16384]{2,1,0:T(1,128)S(1)}, u32[]{:S(2)}, u32[]{:S(2)}) async-start(f32[8,1,16384]{2,1,0:T(1,128)} %reshape.412), calls=%async_computation | async-start | bytes 1048576 | tf_op jit(solution)/shard_map/all_to_all | solution.py:11
  23.9 1.2 copy.53
  25.1 1.0 fusion.111
  26.2 1.2 collective-permute-start
  27.6 1.2 fusion.108
  28.8 0.7 slice_bitcast_fusion.34
  29.5 2.5 %maximum_bitcast_fusion.1 = f32[1,2,32,1,4,32,32]{6,5,4,2,1,3,0:T(8,128)} fusion(f32[1,32,1,4,32,32]{5,4,3,1,0,2:T(8,128)S(1)} %get-tuple-element.52, f32[1,32,1,4,32,32]{5,4,3,1,0,2:T(8,128)S(1)} %get-tuple-element.5), kind=kLoop, calls=%fused_computation.9 | loop fusion | flops 262144 | bytes 2097152 | tf_op jit(solution)/shard_map/stack | solution.py:73
  31.9 0.8 sine_multiply_fusion
  32.7 2.5 %maximum_bitcast_fusion.2 = f32[1,2,32,1,4,32,32]{6,5,4,2,1,3,0:T(8,128)} fusion(f32[1,32,1,4,32,32]{5,4,3,2,1,0:T(8,128)S(1)} %get-tuple-element.6, f32[1,32,1,4,32,32]{5,4,3,2,1,0:T(8,128)S(1)} %slice.210), kind=kLoop, calls=%fused_computation.10 | loop fusion | flops 262144 | bytes 2097152 | tf_op jit(solution)/shard_map/stack | solution.py:73
  35.4 0.6 maximum_bitcast_fusion.7
  36.7 1.9 %reduce = f32[8,16384]{1,0:T(8,128)S(1)} reduce(f32[8,1,16384]{2,1,0:T(1,128)S(1)} %all-to-all-done, f32[]{:T(128)} %broadcast.504), dimensions={1}, to_apply=%all_to_all.14.reduce_sub_computation | reduce | bytes 1048580 | tf_op jit(solution)/shard_map/all_to_all | solution.py:11
  38.6 2.0 %reshape.413 = f32[8,2,4,4,16,32]{5,4,3,2,1,0:T(8,128)} reshape(f32[8,16384]{1,0:T(8,128)S(1)} %reduce) | data formatting | bytes 1048576
  40.6 1.7 %bitcast_bitcast_fusion = f32[2,4,32,4,8,16]{2,5,3,1,0,4:T(8,128)S(1)} fusion(f32[8,2,4,4,16,32]{5,4,3,2,1,0:T(8,128)} %reshape.413), kind=kLoop, calls=%fused_computation.216 | loop fusion | bytes 1048576 | tf_op jit(solution)/shard_map/reshape | solution.py:12
  42.6 3.5 %fusion.55 = f32[2,32,4,4,32]{1,4,0,2,3:T(8,128)S(1)} fusion(f32[2,4,32,4,128,1]{2,4,3,1,0,5:T(8,128)S(1)} %bitcast.217, f32[1,2,32,128]{3,2,1,0:T(8,128)S(1)} %get-tuple-element.55, f32[1,2,32,128]{3,2,1,0:T(8,128)S(1)} %get-tuple-element.56), kind=kOutput, calls=%fused_computation.91 | convolution fusion | flops 100679680 | bytes 720896 | tf_op jit(solution)/shard_map/srny,rkcxy->snxkc/dot_general | solution.py:61
  46.7 0.9 reshape.409
  47.6 14.4 %all-to-all-start.1 = ((f32[2,32,4,128]{3,2,0,1:T(4,128)}), f32[2,32,4,128]{3,2,0,1:T(4,128)S(1)}, u32[]{:S(2)}, u32[]{:S(2)}) async-start(f32[2,32,4,128]{3,2,0,1:T(4,128)} %reshape.409), calls=%async_computation.1 | async-start | bytes 262144 | tf_op jit(solution)/shard_map/all_to_all | solution.py:63
  62.1 1.1 constant_dynamic-update-slice_fusion.2
  63.2 1.2 constant_dynamic-update-slice_fusion.1
  64.4 1.1 constant_dynamic-update-slice_fusion
  65.5 1.7 %copy-done.2 = f32[32,6,16,256]{3,0,2,1:T(8,128)} copy-done((f32[32,6,16,256]{3,0,2,1:T(8,128)}, f32[32,6,16,256]{3,0,2,1:T(8,128)S(1)}, u32[]{:S(2)}) %copy-start.2) | copy-done | bytes 3145752
  67.3 1.1 collective-permute-start.2
  68.4 4.0 %collective-permute-start.3 = (f32[32,6,1,256]{3,0,2,1:T(8,128)S(1)}, f32[32,6,1,256]{3,0,2,1:T(8,128)S(1)}, u32[]{:S(2)}, u32[]{:S(2)}) collective-permute-start(f32[32,6,1,256]{3,0,2,1:T(8,128)S(1)} %get-tuple-element.12), channel_id=1, source_target_pairs={{1,0},{2,1},{3,2},{4,3},{5,4},{6,5},{7,6},{0,7},{9,8},{10,9},{11,1... | collective-permute-start | bytes 589832 | tf_op jit(solution)/shard_map/ppermute | solution.py:23
  72.8 7.2 %fusion = f32[32,4,1,2,32,1]{4,2,5,3,1,0:T(1,128)S(1)} fusion(f32[2,32,4,32,1,1]{3,2,1,0,4,5:T(4,128)S(1)} %reshape.399, f32[1,2,32,1,4,32,32]{6,5,4,2,1,3,0:T(8,128)} %maximum_bitcast_fusion.2, f32[1,2,32,1,4,32,32]{6,5,4,2,1,3,0:T(8,128)} %maximum_bitcast_fusion.1), kind=kOutput, calls=%fused_computation.1 | convolution fusion | flops 6815744 | bytes 2162688 | tf_op jit(solution)/shard_map/rnmki,srmnkio->snmko/dot_general | solution.py:74
  80.6 0.8 copy.67
  81.3 8.8 %all-to-all-start.2 = ((f32[2,1,128,128]{3,0,1,2:T(2,128)}), f32[2,1,128,128]{3,0,1,2:T(2,128)S(1)}, u32[]{:S(2)}, u32[]{:S(2)}) async-start(f32[2,1,128,128]{3,0,1,2:T(2,128)} %copy.67), calls=%async_computation.2 | async-start | bytes 262144 | tf_op jit(solution)/shard_map/all_to_all | solution.py:78
  90.2 1.4 slice_bitcast_fusion.33
  91.6 4.1 %pad_maximum_fusion.1 = f32[32,6,18,256]{3,0,2,1:T(8,128)} fusion(f32[32,6,1,256]{3,0,2,1:T(8,128)S(1)} %collective-permute-done.3, f32[32,6,16,256]{3,0,2,1:T(8,128)} %copy-done.2, f32[32,6,1,256]{3,0,2,1:T(8,128)S(1)} %collective-permute-done.2), kind=kLoop, calls=%fused_computation.11 | loop fusion | flops 1769472 | bytes 7077888 | tf_op jit(solution)/shard_map/concatenate | solution.py:24
  95.7 3.7 %all-to-all-done.2 = f32[2,1,128,128]{3,0,1,2:T(2,128)S(1)} async-done(((f32[2,1,128,128]{3,0,1,2:T(2,128)}), f32[2,1,128,128]{3,0,1,2:T(2,128)S(1)}, u32[]{:S(2)}, u32[]{:S(2)}) %all-to-all-start.2) | async-done | bytes 131104 | tf_op jit(solution)/shard_map/all_to_all | solution.py:78
  100.1 1.1 copy.70
  101.2 3.5 %all-to-all-start.3 = ((f32[2,128,4,128]{3,2,0,1:T(4,128)}), f32[2,128,4,128]{3,2,0,1:T(4,128)S(1)}, u32[]{:S(2)}, u32[]{:S(2)}) async-start(f32[2,128,4,128]{3,2,0,1:T(4,128)} %copy.70), calls=%async_computation.3 | async-start | bytes 1048576 | tf_op jit(solution)/shard_map/all_to_all | solution.py:81
  104.7 2.8 %fusion.109 = (f32[32,6,18,1]{3,0,2,1:T(8,128)S(1)}, f32[32,6,18,1]{3,0,2,1:T(8,128)S(1)}) fusion(f32[32,6,18,256]{3,0,2,1:T(8,128)} %pad_maximum_fusion.1), kind=kLoop, calls=%fused_computation.213 | loop fusion | bytes 55296 | tf_op jit(solution)/shard_map/slice | solution.py:87
  107.7 5.5 %maximum_maximum_fusion = (f32[32,6,18,257]{3,0,2,1:T(8,128)}, f32[32,6,18,257]{3,0,2,1:T(8,128)}) fusion(f32[32,6,1,256]{3,0,2,1:T(8,128)S(1)} %collective-permute-done.3, f32[32,6,16,256]{3,0,2,1:T(8,128)S(1)} %copy-done.3, f32[32,6,1,256]{3,0,2,1:T(8,128)S(1)} %collective-permute-done.2, f32[32,6,18,1]{3,0,2,1:T(8,128)S(1)} %get-tuple-element.9, ...), kind=kLoop, calls=%fused_computation.3 | loop fusion | flops 5329152 | bytes 10672128 | tf_op jit(solution)/shard_map/concatenate | solution.py:87
  113.2 2.3 %all-to-all-done.3 = f32[2,128,4,128]{3,2,0,1:T(4,128)S(1)} async-done(((f32[2,128,4,128]{3,2,0,1:T(4,128)}), f32[2,128,4,128]{3,2,0,1:T(4,128)S(1)}, u32[]{:S(2)}, u32[]{:S(2)}) %all-to-all-start.3) | async-done | bytes 524320 | tf_op jit(solution)/shard_map/all_to_all | solution.py:81
  115.8 1.8 %reshape.391 = f32[2,16,4,32,32]{4,3,2,1,0:T(8,128)} reshape(f32[2,16,4,8,128]{4,3,2,1,0:T(8,128)S(1)} %bitcast.218) | data formatting | bytes 1048576 | tf_op jit(solution)/shard_map/reshape | solution.py:84
  117.8 5.3 %fusion.72 = f32[16,4,32,256,1]{3,2,1,0,4:T(8,128)S(1)} fusion(f32[2,16,4,32,32]{4,3,2,1,0:T(8,128)} %reshape.391, f32[1,32,256]{2,1,0:T(8,128)} %get-tuple-element.57, f32[1,32,256]{2,1,0:T(8,128)} %get-tuple-element.58), kind=kOutput, calls=%fused_computation.123 | convolution fusion | flops 402669568 | bytes 2686976 | tf_op jit(solution)/shard_map/skz,syxkc->cxyz/dot_general | solution.py:85
  123.4 21.7 %fusion.8 = f32[32,4,16,256]{3,0,2,1:T(8,128)S(1)} fusion(f32[32,6,18,257]{3,0,2,1:T(8,128)} %get-tuple-element.8, f32[32,6,1,256]{3,0,2,1:T(8,128)S(1)} %collective-permute-done.3, f32[32,6,16,256]{3,0,2,1:T(8,128)S(1)} %copy-done.4, f32[32,6,18,257]{3,0,2,1:T(8,128)} %get-tuple-element.7, f32[32,1,16,256]{3,0,2,1:T(8,128)} %collective-permute-done.1, ...), kind=kOutput, calls=%fused_computation.23 | convolution fusion | flops 239075328 | bytes 50732544 | tf_op jit(solution)/shard_map/dot_general | solution.py:103
  145.1 2.5 %copy.81 = f32[32,4,16,256]{3,2,1,0:T(8,128)} copy(f32[32,4,16,256]{3,0,2,1:T(8,128)S(1)} %fusion.8) | data formatting | bytes 4194304 | tf_op jit(solution)/shard_map/mul | solution.py:107
  (110 shorter events, 4.2 us)
Async XLA Ops:
  0.0 123.1 %copy-start = (f32[32,32]{1,0:T(8,128)S(1)}, f32[32,32]{1,0:T(8,128)}, u32[]{:S(2)}) copy-start(f32[32,32]{1,0:T(8,128)} %param.8) | copy-start | bytes 12292
  6.3 4.4 %copy-start.6 = (f32[64,32,4,16]{1,3,2,0:T(8,128)}, f32[64,32,4,16]{1,3,2,0:T(8,128)S(1)}, u32[]{:S(2)}) copy-start(f32[64,32,4,16]{1,3,2,0:T(8,128)S(1)} %copy.103) | copy-start | bytes 1572868
  11.4 12.4 %copy-start.1 = (f32[32,4,16,256]{3,2,1,0:T(8,128)S(1)}, f32[32,4,16,256]{3,2,1,0:T(8,128)}, u32[]{:S(2)}) copy-start(f32[32,4,16,256]{3,2,1,0:T(8,128)} %param.5) | copy-start | bytes 6291460
  16.4 19.7 %all-to-all-start = ((f32[8,1,16384]{2,1,0:T(1,128)}), f32[8,1,16384]{2,1,0:T(1,128)S(1)}, u32[]{:S(2)}, u32[]{:S(2)}) async-start(f32[8,1,16384]{2,1,0:T(1,128)} %reshape.412), calls=%async_computation | async-start | bytes 1048576 | tf_op jit(solution)/shard_map/all_to_all | solution.py:11
  23.9 3.5 %copy-start.5 = (f32[2,32,1,4,32,32]{5,4,3,2,1,0:T(8,128)S(1)}, f32[2,32,1,4,32,32]{5,4,3,2,1,0:T(8,128)}, u32[]{:S(2)}) copy-start(f32[2,32,1,4,32,32]{5,4,3,2,1,0:T(8,128)} %param.6) | copy-start | bytes 3145732
  26.2 35.9 %collective-permute-start = (f32[32,1,16,256]{3,0,2,1:T(8,128)}, f32[32,1,16,256]{3,0,2,1:T(8,128)}, u32[]{:S(2)}, u32[]{:S(2)}) collective-permute-start(f32[32,1,16,256]{3,0,2,1:T(8,128)} %get-tuple-element.14), channel_id=1, source_target_pairs={{0,8},{8,16},{16,24},{24,32},{32,40},{40,48},{48,56},{56,64},{64,7... | collective-permute-start | bytes 1572872 | tf_op jit(solution)/shard_map/ppermute | solution.py:22
  27.3 37.1 %collective-permute-start.1 = (f32[32,1,16,256]{3,0,2,1:T(8,128)}, f32[32,1,16,256]{3,0,2,1:T(8,128)}, u32[]{:S(2)}, u32[]{:S(2)}) collective-permute-start(f32[32,1,16,256]{3,0,2,1:T(8,128)} %get-tuple-element.13), channel_id=1, source_target_pairs={{8,0},{16,8},{24,16},{32,24},{40,32},{48,40},{56,48},{64,56},{72,6... | collective-permute-start | bytes 1572872 | tf_op jit(solution)/shard_map/ppermute | solution.py:23
  36.0 6.6 %copy-start.8 = (f32[1,2,32,128]{3,2,1,0:T(8,128)}, f32[1,2,32,128]{3,2,1,0:T(8,128)S(1)}, u32[]{:S(2)}) copy-start(f32[1,2,32,128]{3,2,1,0:T(8,128)S(1)} %get-tuple-element.55) | copy-start | bytes 98308
  36.0 6.6 %copy-start.10 = (f32[1,2,32,128]{3,2,1,0:T(8,128)}, f32[1,2,32,128]{3,2,1,0:T(8,128)S(1)}, u32[]{:S(2)}) copy-start(f32[1,2,32,128]{3,2,1,0:T(8,128)S(1)} %get-tuple-element.56) | copy-start | bytes 98308
  47.6 24.8 %all-to-all-start.1 = ((f32[2,32,4,128]{3,2,0,1:T(4,128)}), f32[2,32,4,128]{3,2,0,1:T(4,128)S(1)}, u32[]{:S(2)}, u32[]{:S(2)}) async-start(f32[2,32,4,128]{3,2,0,1:T(4,128)} %reshape.409), calls=%async_computation.1 | async-start | bytes 262144 | tf_op jit(solution)/shard_map/all_to_all | solution.py:63
  64.4 8.1 %copy-start.9 = (f32[1,2,32,128]{3,2,1,0:T(8,128)S(1)}, f32[1,2,32,128]{3,2,1,0:T(8,128)}, u32[]{:S(2)}) copy-start(f32[1,2,32,128]{3,2,1,0:T(8,128)} %copy-done.8) | copy-start | bytes 98308
  64.4 8.1 %copy-start.11 = (f32[1,2,32,128]{3,2,1,0:T(8,128)S(1)}, f32[1,2,32,128]{3,2,1,0:T(8,128)}, u32[]{:S(2)}) copy-start(f32[1,2,32,128]{3,2,1,0:T(8,128)} %copy-done.10) | copy-start | bytes 98308
  67.3 24.3 %collective-permute-start.2 = (f32[32,6,1,256]{3,0,2,1:T(8,128)S(1)}, f32[32,6,1,256]{3,0,2,1:T(8,128)S(1)}, u32[]{:S(2)}, u32[]{:S(2)}) collective-permute-start(f32[32,6,1,256]{3,0,2,1:T(8,128)S(1)} %get-tuple-element.11), channel_id=1, source_target_pairs={{0,1},{1,2},{2,3},{3,4},{4,5},{5,6},{6,7},{7,0},{8,9},{9,10},{10,1... | collective-permute-start | bytes 589832 | tf_op jit(solution)/shard_map/ppermute | solution.py:22
  68.4 23.2 %collective-permute-start.3 = (f32[32,6,1,256]{3,0,2,1:T(8,128)S(1)}, f32[32,6,1,256]{3,0,2,1:T(8,128)S(1)}, u32[]{:S(2)}, u32[]{:S(2)}) collective-permute-start(f32[32,6,1,256]{3,0,2,1:T(8,128)S(1)} %get-tuple-element.12), channel_id=1, source_target_pairs={{1,0},{2,1},{3,2},{4,3},{5,4},{6,5},{7,6},{0,7},{9,8},{10,9},{11,1... | collective-permute-start | bytes 589832 | tf_op jit(solution)/shard_map/ppermute | solution.py:23
  72.8 7.4 %copy-start.12 = (f32[1,2,32,128]{3,2,1,0:T(8,128)S(1)}, f32[1,2,32,128]{3,2,1,0:T(8,128)}, u32[]{:S(2)}) copy-start(f32[1,2,32,128]{3,2,1,0:T(8,128)} %get-tuple-element.42) | copy-start | bytes 98308
  72.8 7.4 %copy-start.13 = (f32[1,2,32,128]{3,2,1,0:T(8,128)S(1)}, f32[1,2,32,128]{3,2,1,0:T(8,128)}, u32[]{:S(2)}) copy-start(f32[1,2,32,128]{3,2,1,0:T(8,128)} %get-tuple-element.43) | copy-start | bytes 98308
  81.3 18.1 %all-to-all-start.2 = ((f32[2,1,128,128]{3,0,1,2:T(2,128)}), f32[2,1,128,128]{3,0,1,2:T(2,128)S(1)}, u32[]{:S(2)}, u32[]{:S(2)}) async-start(f32[2,1,128,128]{3,0,1,2:T(2,128)} %copy.67), calls=%async_computation.2 | async-start | bytes 262144 | tf_op jit(solution)/shard_map/all_to_all | solution.py:78
  101.2 14.2 %all-to-all-start.3 = ((f32[2,128,4,128]{3,2,0,1:T(4,128)}), f32[2,128,4,128]{3,2,0,1:T(4,128)S(1)}, u32[]{:S(2)}, u32[]{:S(2)}) async-start(f32[2,128,4,128]{3,2,0,1:T(4,128)} %copy.70), calls=%async_computation.3 | async-start | bytes 1048576 | tf_op jit(solution)/shard_map/all_to_all | solution.py:81
  104.7 3.0 %copy-start.3 = (f32[32,6,16,256]{3,0,2,1:T(8,128)S(1)}, f32[32,6,16,256]{3,0,2,1:T(8,128)}, u32[]{:S(2)}) copy-start(f32[32,6,16,256]{3,0,2,1:T(8,128)} %copy-done.2) | copy-start | bytes 9437188
  117.6 5.6 %copy-start.4 = (f32[32,6,16,256]{3,0,2,1:T(8,128)S(1)}, f32[32,6,16,256]{3,0,2,1:T(8,128)}, u32[]{:S(2)}) copy-start(f32[32,6,16,256]{3,0,2,1:T(8,128)} %copy-done.2) | copy-start | bytes 9437188
  117.6 5.6 %copy-start.15 = (f32[32]{0:T(128)S(1)}, f32[32]{0:T(128)}, u32[]{:S(2)}) copy-start(f32[32]{0:T(128)} %get-tuple-element.15) | copy-start | bytes 388
  117.6 5.6 %copy-start.16 = (f32[32]{0:T(128)S(1)}, f32[32]{0:T(128)}, u32[]{:S(2)}) copy-start(f32[32]{0:T(128)} %get-tuple-element.16) | copy-start | bytes 388
  117.6 5.6 %copy-start.17 = (f32[32]{0:T(128)S(1)}, f32[32]{0:T(128)}, u32[]{:S(2)}) copy-start(f32[32]{0:T(128)} %get-tuple-element.17) | copy-start | bytes 388
  117.6 5.6 %copy-start.18 = (f32[32]{0:T(128)S(1)}, f32[32]{0:T(128)}, u32[]{:S(2)}) copy-start(f32[32]{0:T(128)} %get-tuple-element.18) | copy-start | bytes 388
  117.6 5.6 %copy-start.19 = (f32[32]{0:T(128)S(1)}, f32[32]{0:T(128)}, u32[]{:S(2)}) copy-start(f32[32]{0:T(128)} %get-tuple-element.19) | copy-start | bytes 388
  117.6 5.6 %copy-start.20 = (f32[32]{0:T(128)S(1)}, f32[32]{0:T(128)}, u32[]{:S(2)}) copy-start(f32[32]{0:T(128)} %get-tuple-element.20) | copy-start | bytes 388
  117.6 5.6 %copy-start.21 = (f32[32]{0:T(128)S(1)}, f32[32]{0:T(128)}, u32[]{:S(2)}) copy-start(f32[32]{0:T(128)} %get-tuple-element.21) | copy-start | bytes 388
  117.6 5.6 %copy-start.22 = (f32[32]{0:T(128)S(1)}, f32[32]{0:T(128)}, u32[]{:S(2)}) copy-start(f32[32]{0:T(128)} %get-tuple-element.22) | copy-start | bytes 388
  117.6 5.6 %copy-start.23 = (f32[32]{0:T(128)S(1)}, f32[32]{0:T(128)}, u32[]{:S(2)}) copy-start(f32[32]{0:T(128)} %get-tuple-element.23) | copy-start | bytes 388
  117.6 5.6 %copy-start.24 = (f32[32]{0:T(128)S(1)}, f32[32]{0:T(128)}, u32[]{:S(2)}) copy-start(f32[32]{0:T(128)} %get-tuple-element.24) | copy-start | bytes 388
  117.6 5.6 %copy-start.25 = (f32[32]{0:T(128)S(1)}, f32[32]{0:T(128)}, u32[]{:S(2)}) copy-start(f32[32]{0:T(128)} %get-tuple-element.25) | copy-start | bytes 388
  117.6 5.6 %copy-start.26 = (f32[32]{0:T(128)S(1)}, f32[32]{0:T(128)}, u32[]{:S(2)}) copy-start(f32[32]{0:T(128)} %get-tuple-element.26) | copy-start | bytes 388
  117.7 5.6 %copy-start.27 = (f32[32]{0:T(128)S(1)}, f32[32]{0:T(128)}, u32[]{:S(2)}) copy-start(f32[32]{0:T(128)} %get-tuple-element.27) | copy-start | bytes 388
  117.7 5.6 %copy-start.28 = (f32[32]{0:T(128)S(1)}, f32[32]{0:T(128)}, u32[]{:S(2)}) copy-start(f32[32]{0:T(128)} %get-tuple-element.28) | copy-start | bytes 388
  117.7 5.6 %copy-start.29 = (f32[32]{0:T(128)S(1)}, f32[32]{0:T(128)}, u32[]{:S(2)}) copy-start(f32[32]{0:T(128)} %get-tuple-element.29) | copy-start | bytes 388
  117.7 5.6 %copy-start.30 = (f32[32]{0:T(128)S(1)}, f32[32]{0:T(128)}, u32[]{:S(2)}) copy-start(f32[32]{0:T(128)} %get-tuple-element.30) | copy-start | bytes 388
  117.7 5.6 %copy-start.31 = (f32[32]{0:T(128)S(1)}, f32[32]{0:T(128)}, u32[]{:S(2)}) copy-start(f32[32]{0:T(128)} %get-tuple-element.31) | copy-start | bytes 388
  117.7 5.6 %copy-start.32 = (f32[32]{0:T(128)S(1)}, f32[32]{0:T(128)}, u32[]{:S(2)}) copy-start(f32[32]{0:T(128)} %get-tuple-element.32) | copy-start | bytes 388
  117.7 5.6 %copy-start.33 = (f32[32]{0:T(128)S(1)}, f32[32]{0:T(128)}, u32[]{:S(2)}) copy-start(f32[32]{0:T(128)} %get-tuple-element.33) | copy-start | bytes 388
  117.7 5.6 %copy-start.34 = (f32[32]{0:T(128)S(1)}, f32[32]{0:T(128)}, u32[]{:S(2)}) copy-start(f32[32]{0:T(128)} %get-tuple-element.34) | copy-start | bytes 388
  117.7 5.6 %copy-start.35 = (f32[32]{0:T(128)S(1)}, f32[32]{0:T(128)}, u32[]{:S(2)}) copy-start(f32[32]{0:T(128)} %get-tuple-element.35) | copy-start | bytes 388
  117.7 5.6 %copy-start.36 = (f32[32]{0:T(128)S(1)}, f32[32]{0:T(128)}, u32[]{:S(2)}) copy-start(f32[32]{0:T(128)} %get-tuple-element.36) | copy-start | bytes 388
  117.8 5.6 %copy-start.37 = (f32[32]{0:T(128)S(1)}, f32[32]{0:T(128)}, u32[]{:S(2)}) copy-start(f32[32]{0:T(128)} %get-tuple-element.37) | copy-start | bytes 388
  117.8 5.6 %copy-start.38 = (f32[32]{0:T(128)S(1)}, f32[32]{0:T(128)}, u32[]{:S(2)}) copy-start(f32[32]{0:T(128)} %get-tuple-element.38) | copy-start | bytes 388
  117.8 5.6 %copy-start.39 = (f32[32]{0:T(128)S(1)}, f32[32]{0:T(128)}, u32[]{:S(2)}) copy-start(f32[32]{0:T(128)} %get-tuple-element.39) | copy-start | bytes 388
  117.8 5.6 %copy-start.40 = (f32[32]{0:T(128)S(1)}, f32[32]{0:T(128)}, u32[]{:S(2)}) copy-start(f32[32]{0:T(128)} %get-tuple-element.40) | copy-start | bytes 388
  117.8 5.6 %copy-start.41 = (f32[32]{0:T(128)S(1)}, f32[32]{0:T(128)}, u32[]{:S(2)}) copy-start(f32[32]{0:T(128)} %get-tuple-element.41) | copy-start | bytes 388
  117.8 5.6 %copy-start.42 = (f32[32]{0:T(128)S(1)}, f32[32]{0:T(128)}, u32[]{:S(2)}) copy-start(f32[32]{0:T(128)} %param.9) | copy-start | bytes 388
  (3 other events, 5.4 us)
